TPU v7x, 32 devices: a whole 2x2x4 slice. The times are simulated.
32 devices in a mesh: grp: 2 (over x), lon: 8 (over z, y), lat: 2 (over core).
Axes of the slice: x: 2, y: 2, z: 4, core: 2. Of those that a mesh axis runs over, the one named last changes fastest.
Arguments:
- cloud_state: float32 [4, 256, 128, 1024], P('grp', 'lon', 'lat'), parts along dimension 0, may hold values from -6 to 6
- counts: int32 [512, 128], P(('grp', 'lon'), 'lat'), parts along dimension 0, may hold values from 1 to 8, as said below
- courant: float32 [32], replicated, may hold values from 0.2 to 0.9
- truncation: int32 [96], replicated, may hold values from 0 to 94, as said below
Outputs:
- cloud_next: float32 [4, 256, 128, 1024], P('grp', 'lon', 'lat'), parts along dimension 0
There are 2 independent parts, one for each index of `grp`. A program takes and returns all parts, laid end to end along the dimension named above; an argument that names none is the same for every part. Nothing has to cross between parts.
Inputs may be any that keep to these rules, and one draw needn't show every extreme that they name: `counts`: columns come in busy regions of 4 to 8 substeps and calm ones of 1 or 2; column 0, 0 has 8. truncation[m] lies in m .. 85 for m <= 85, truncation[0] = 85, and truncation[m] = m - 1 (nothing kept) for m > 85.
All inputs are finite; a program needn't handle non-finite values.
Results may differ from a plain program's by a relative error of at most 0.0003.
Values sent between devices are 32-bit elements; how exact they have to be, the bound alone decides.
No kernel may reach another device: no remote copies, remote signals or barrier semaphores. Data moves between devices by JAX's collectives and lax.ppermute only.
A program may use at most 64 MiB of HBM per device.

v0:
```python
import jax
import jax.numpy as jnp
from jax import lax
from jax.sharding import PartitionSpec as P

NN = 96
couple_gain = 8.0


def legendre(orders, lat_rows, lat_total, degrees):
    latitude = -0.5 * jnp.pi + jnp.pi * (lat_rows.astype(jnp.float32) + 0.5) / lat_total
    sin_lat = jnp.sin(latitude)
    cos_lat = jnp.cos(latitude)
    order_f = orders.astype(jnp.float32)
    ladder = jnp.arange(1, degrees + 1).astype(jnp.float32)
    log_gains = 0.5 * jnp.log((2.0 * ladder + 1.0) / (2.0 * ladder))
    included = (ladder[None, :] <= order_f[:, None]).astype(jnp.float32)
    log_start = 0.5 * jnp.log(jnp.float32(0.5)) + jnp.sum(included * log_gains[None, :], axis=1)
    diagonal = jnp.exp(log_start[:, None] + order_f[:, None] * jnp.log(cos_lat)[None, :])

    def legendre_advance(carry, degree):
        previous, earlier, inverse = carry
        degree_f = degree.astype(jnp.float32)
        higher = degree_f > order_f
        numerator = jnp.maximum(4.0 * degree_f * degree_f - 1.0, 1.0)
        denominator = jnp.where(higher, degree_f * degree_f - order_f * order_f, 1.0)
        factor = jnp.sqrt(numerator / denominator)
        raised = factor[:, None] * (sin_lat[None, :] * previous - inverse[:, None] * earlier)
        current = jnp.where(
            (degree_f == order_f)[:, None], diagonal, jnp.where(higher[:, None], raised, 0.0)
        )
        return ((current, previous, jnp.where(higher, 1.0 / factor, 0.0)), current)

    initial = (jnp.zeros_like(diagonal), jnp.zeros_like(diagonal), jnp.zeros_like(order_f))
    _, stacked = lax.scan(legendre_advance, initial, jnp.arange(degrees, dtype=jnp.int32), unroll=8)
    return jnp.transpose(stacked, (1, 0, 2))


def latitude_weights(lat_rows, lat_total):
    latitude = -0.5 * jnp.pi + jnp.pi * (lat_rows.astype(jnp.float32) + 0.5) / lat_total
    return jnp.pi * jnp.cos(latitude) / lat_total


def wave_table(lon_rows, modes, lon_total):
    phase = lon_rows[:, None] * modes[None, :] % lon_total
    angle = phase.astype(jnp.float32) * (2.0 * jnp.pi / lon_total)
    return (jnp.cos(angle), jnp.sin(angle))


def substep(theta, moist, force, count, index, rate, profile, levels):
    heated = theta + couple_gain * profile[None, None, :] * force[:, :, None]
    moved_theta = heated - rate * (heated - jnp.roll(heated, levels, axis=2))
    moved_moist = moist - rate * (moist - jnp.roll(moist, levels, axis=2))
    excess = moved_moist - (1.0 + 0.2 * moved_theta)
    condensed = 0.25 * (excess + jnp.sqrt(excess * excess + 0.01))
    active = (index < count)[:, :, None]
    return (
        jnp.where(active, moved_theta + 0.5 * condensed, theta),
        jnp.where(active, moved_moist - condensed, moist),
    )


def run_block(block_state, force_rows, count_rows, rate, profile, levels, trip_count):

    def unfinished(carry):
        return carry[0] < trip_count

    def run_advance(carry):
        index, theta, moist = carry
        theta, moist = substep(theta, moist, force_rows, count_rows, index, rate, profile, levels)
        return (index + 1, theta, moist)

    _, theta, moist = lax.while_loop(
        unfinished, run_advance, (jnp.int32(0), block_state[0], block_state[1])
    )
    return jnp.stack([theta, moist])


def shards(cloud_state, counts, courant, truncation):
    highest = lax.Precision.HIGHEST
    lon_devices = lax.axis_size("lon")
    lon_index = lax.axis_index("lon")
    lat_index = lax.axis_index("lat")
    fields, lon_local, lat_local, cells = cloud_state.shape
    levels = courant.shape[0]
    columns_across = cells // levels
    total_lon = lon_local * lon_devices
    total_lat = lat_local * lax.axis_size("lat")
    total_modes = truncation.shape[0]
    mode_local = total_modes // lon_devices
    heating = jnp.mean(cloud_state[0], axis=2)
    my_lons = lon_index * lon_local + jnp.arange(lon_local, dtype=jnp.int32)
    modes = jnp.arange(mode_local * lax.axis_size("lon"), dtype=jnp.int32)
    cosine_table, sine_table = wave_table(my_lons, modes, total_lon)
    coefs = lax.psum_scatter(
        jnp.stack(
            [
                jnp.dot(cosine_table.T, heating, precision=highest),
                jnp.dot(sine_table.T, heating, precision=highest),
            ],
            1,
        )
        / total_lon,
        "lon",
        scatter_dimension=0,
        tiled=True,
    )
    my_modes = lon_index * mode_local + jnp.arange(mode_local, dtype=jnp.int32)
    my_lats = lat_index * lat_local + jnp.arange(lat_local, dtype=jnp.int32)
    table = legendre(my_modes, my_lats, total_lat, NN)
    weights = latitude_weights(my_lats, total_lat)
    partial_spec = jnp.einsum(
        "mnj,mcj->mcn", table, coefs * weights[None, None, :], precision=highest
    )
    spectrum = lax.psum(partial_spec, "lat")
    my_trunc = lax.dynamic_slice_in_dim(truncation, lon_index * mode_local, mode_local)
    degrees = jnp.arange(NN, dtype=jnp.int32)
    keep_mask = (
        (degrees[None, :] >= my_modes[:, None]) & (degrees[None, :] <= my_trunc[:, None])
    ).astype(jnp.float32)
    filtered = jnp.einsum(
        "mnj,mcn->mcj", table, spectrum * keep_mask[:, None, :], precision=highest
    )
    piece = lax.all_gather(filtered, "lon", axis=0, tiled=True)
    modes = jnp.arange(piece.shape[0], dtype=jnp.int32)
    cosine_table, sine_table = wave_table(my_lons, modes, total_lon)
    factor = jnp.where(modes == 0, 1.0, 2.0).astype(jnp.float32)[:, None]
    forcing = jnp.dot(cosine_table, factor * piece[:, 0], precision=highest) + jnp.dot(
        sine_table, factor * piece[:, 1], precision=highest
    )
    level_profile = jnp.sin(jnp.pi * (jnp.arange(levels).astype(jnp.float32) + 0.5) / levels)
    profile = jnp.tile(level_profile, columns_across)
    rate = jnp.tile(courant, columns_across)[None, None, :]
    blocks_count = 8
    block_rows = lon_local // blocks_count
    block_cost = jnp.max(counts.reshape(blocks_count, block_rows, lat_local), axis=(1, 2))

    def visit(block_index, updated):
        start = block_index * block_rows
        piece = lax.dynamic_slice_in_dim(cloud_state, start, block_rows, 1)
        force_rows = lax.dynamic_slice_in_dim(forcing, start, block_rows, 0)
        count_rows = lax.dynamic_slice_in_dim(counts, start, block_rows, 0)
        result = run_block(
            piece, force_rows, count_rows, rate, profile, levels, block_cost[block_index]
        )
        return lax.dynamic_update_slice_in_dim(updated, result, start, 1)

    updated = lax.fori_loop(0, blocks_count, visit, cloud_state)
    return updated


def solution(mesh):
    return jax.shard_map(
        shards,
        mesh=mesh,
        in_specs=(P("grp", "lon", "lat", None), P(("grp", "lon"), "lat"), P(), P()),
        out_specs=P("grp", "lon", "lat", None),
        check_vma=False,
    )
```

profile of v0, /device:TPU:8, one launch (start us, length us, event | category | flops | bytes accessed | tf_op | source)
XLA Modules:
  0.0 384.5 jit_solution(14909525809693610050)
XLA Ops:
  4.3 3.8 slice_reduce_fusion
  8.8 35.5 %all-reduce = f32[96,2,64]{2,1,0:T(2,128)S(1)} all-reduce(f32[96,2,64]{2,1,0:T(2,128)S(1)} %copy.12), channel_id=2, replica_groups=mesh['grp'=2,'lon'=8,'lat'=2] {'lon'}, use_global_device_ids=true, to_apply=%region_1.2.clone | all-reduce | flops 12288 | bytes 98304
  44.4 82.5 %while.81 = (s32[]{:T(128)}, f32[12,64]{1,0:T(8,128)S(1)}, f32[12,64]{1,0:T(8,128)S(1)}, f32[12]{0:T(128)S(1)}, f32[12,8,12,64]{3,2,1,0:T(8,128)S(1)}, /*index=5...) while((s32[]{:T(128)}, f32[12,64]{1,0:T(8,128)S(1)}, ...), condition=%wide.region_4.5_spmd.clone.clone.clone, body=%wide.region_3.4_spmd.clone.clone.clone.sunk | while | flops 108922 | bytes 421596 | solution.py:35
  127.6 3.3 psum.7
  131.6 30.6 %all_gather.3 = f32[96,2,64]{2,1,0:T(2,128)S(1)} all-gather(f32[12,2,64]{2,1,0:T(2,128)S(1)} %fusion.42), channel_id=1, replica_groups=mesh['grp'=2,'lon'=8,'lat'=2] {'lon'}, dimensions={0}, use_global_device_ids=true | all-gather | bytes 55296 | tf_op jit(solution)/shard_map/all_gather | solution.py:124
  162.8 12.0 %copy.50 = f32[2,32,64,1024]{3,2,1,0:T(8,128)} copy(f32[2,32,64,1024]{3,2,1,0:T(8,128)} %param.10) | data formatting | bytes 33554432
  174.8 209.7 %while.80 = (s32[]{:T(128)}, f32[2,32,64,1024]{3,2,1,0:T(8,128)}, f32[2,32,64,1024]{3,2,1,0:T(8,128)}, s32[8]{0:T(128)S(1)}, f32[32,64]{1,0:T(8,128)S(1)}, /*ind...) while((s32[]{:T(128)}, f32[2,32,64,1024]{3,2,1,0:T(8,128)}, ...), condition=%wide.region_11.12_spmd.clone, body=%wide.region_8.11_spmd.clone.sunk | while | flops 6817033 | bytes 18993312 | solution.py:148
  176.2 1.7 dynamic-slice_bitcast_fusion.3
  177.9 21.7 %while.82 = (s32[]{:T(128)}, f32[4,64,1024]{2,1,0:T(8,128)S(1)}, f32[4,64,1024]{2,1,0:T(8,128)S(1)}, s32[]{:T(128)}, s32[4,64]{1,0:T(4,128)S(1)}, /*index=5*/f32...) while((s32[]{:T(128)}, f32[4,64,1024]{2,1,0:T(8,128)S(1)}, ...), condition=%wide.region_10.10_spmd, body=%wide.region_9.9_spmd.sunk | while | flops 6292738 | bytes 10583657 | solution.py:73
  179.1 1.4 subtract_select_fusion.2
  199.6 1.5 maximum_dynamic-update-slice_fusion.2
  202.4 1.7 dynamic-slice_bitcast_fusion.3
  204.1 21.7 %while.82 = (s32[]{:T(128)}, f32[4,64,1024]{2,1,0:T(8,128)S(1)}, f32[4,64,1024]{2,1,0:T(8,128)S(1)}, s32[]{:T(128)}, s32[4,64]{1,0:T(4,128)S(1)}, /*index=5*/f32...) while((s32[]{:T(128)}, f32[4,64,1024]{2,1,0:T(8,128)S(1)}, ...), condition=%wide.region_10.10_spmd, body=%wide.region_9.9_spmd.sunk | while | flops 6292738 | bytes 10583657 | solution.py:73
  225.8 1.5 maximum_dynamic-update-slice_fusion.2
  228.6 1.7 dynamic-slice_bitcast_fusion.3
  230.3 21.7 %while.82 = (s32[]{:T(128)}, f32[4,64,1024]{2,1,0:T(8,128)S(1)}, f32[4,64,1024]{2,1,0:T(8,128)S(1)}, s32[]{:T(128)}, s32[4,64]{1,0:T(4,128)S(1)}, /*index=5*/f32...) while((s32[]{:T(128)}, f32[4,64,1024]{2,1,0:T(8,128)S(1)}, ...), condition=%wide.region_10.10_spmd, body=%wide.region_9.9_spmd.sunk | while | flops 6292738 | bytes 10583657 | solution.py:73
  252.0 1.5 maximum_dynamic-update-slice_fusion.2
  254.8 1.7 dynamic-slice_bitcast_fusion.3
  256.5 21.7 %while.82 = (s32[]{:T(128)}, f32[4,64,1024]{2,1,0:T(8,128)S(1)}, f32[4,64,1024]{2,1,0:T(8,128)S(1)}, s32[]{:T(128)}, s32[4,64]{1,0:T(4,128)S(1)}, /*index=5*/f32...) while((s32[]{:T(128)}, f32[4,64,1024]{2,1,0:T(8,128)S(1)}, ...), condition=%wide.region_10.10_spmd, body=%wide.region_9.9_spmd.sunk | while | flops 6292738 | bytes 10583657 | solution.py:73
  278.2 1.5 maximum_dynamic-update-slice_fusion.2
  281.0 1.7 dynamic-slice_bitcast_fusion.3
  282.7 21.7 %while.82 = (s32[]{:T(128)}, f32[4,64,1024]{2,1,0:T(8,128)S(1)}, f32[4,64,1024]{2,1,0:T(8,128)S(1)}, s32[]{:T(128)}, s32[4,64]{1,0:T(4,128)S(1)}, /*index=5*/f32...) while((s32[]{:T(128)}, f32[4,64,1024]{2,1,0:T(8,128)S(1)}, ...), condition=%wide.region_10.10_spmd, body=%wide.region_9.9_spmd.sunk | while | flops 6292738 | bytes 10583657 | solution.py:73
  304.4 1.5 maximum_dynamic-update-slice_fusion.2
  307.3 1.7 dynamic-slice_bitcast_fusion.3
  308.9 21.7 %while.82 = (s32[]{:T(128)}, f32[4,64,1024]{2,1,0:T(8,128)S(1)}, f32[4,64,1024]{2,1,0:T(8,128)S(1)}, s32[]{:T(128)}, s32[4,64]{1,0:T(4,128)S(1)}, /*index=5*/f32...) while((s32[]{:T(128)}, f32[4,64,1024]{2,1,0:T(8,128)S(1)}, ...), condition=%wide.region_10.10_spmd, body=%wide.region_9.9_spmd.sunk | while | flops 6292738 | bytes 10583657 | solution.py:73
  330.6 1.5 maximum_dynamic-update-slice_fusion.2
  333.5 1.7 dynamic-slice_bitcast_fusion.3
  335.2 21.7 %while.82 = (s32[]{:T(128)}, f32[4,64,1024]{2,1,0:T(8,128)S(1)}, f32[4,64,1024]{2,1,0:T(8,128)S(1)}, s32[]{:T(128)}, s32[4,64]{1,0:T(4,128)S(1)}, /*index=5*/f32...) while((s32[]{:T(128)}, f32[4,64,1024]{2,1,0:T(8,128)S(1)}, ...), condition=%wide.region_10.10_spmd, body=%wide.region_9.9_spmd.sunk | while | flops 6292738 | bytes 10583657 | solution.py:73
  356.9 1.5 maximum_dynamic-update-slice_fusion.2
  359.7 1.7 dynamic-slice_bitcast_fusion.3
  361.4 21.7 %while.82 = (s32[]{:T(128)}, f32[4,64,1024]{2,1,0:T(8,128)S(1)}, f32[4,64,1024]{2,1,0:T(8,128)S(1)}, s32[]{:T(128)}, s32[4,64]{1,0:T(4,128)S(1)}, /*index=5*/f32...) while((s32[]{:T(128)}, f32[4,64,1024]{2,1,0:T(8,128)S(1)}, ...), condition=%wide.region_10.10_spmd, body=%wide.region_9.9_spmd.sunk | while | flops 6292738 | bytes 10583657 | solution.py:73
  383.1 1.5 maximum_dynamic-update-slice_fusion.2
  (941 shorter events, 160.9 us)
Async XLA Ops:
  162.8 12.0 %copy-start = (f32[32]{0:T(128)S(1)}, f32[32]{0:T(128)}, u32[]{:S(2)}) copy-start(f32[32]{0:T(128)} %param.12) | copy-start | bytes 388
where the time goes:
time: 387 us; the launch traced here: 385 us
  other arithmetic  131 us (34%)
  loops' own time  111 us (29%)
  local copies, waits for them, and re-layouts  70.2 us (18%)
  blocking collectives  69.3 us (18%)
    select_n x64, other arithmetic, substep(): jnp.where(active, moved_moist - condensed, moist)  91.4 us
    another operation x1, loops' own time, legendre(): lax.scan(legendre_advance, initial, jnp.arange(degrees, dtype=jnp.int32),...  62.2 us
    another operation x8, loops' own time, run_block(): lax.while_loop(unfinished, run_advance, (jnp.int32(0), block_state[0], bl...  48.8 us
    unnamed x1, blocking collectives  35.5 us
    all_gather x1, blocking collectives, shards(): piece = lax.all_gather(filtered, 'lon', axis=0, tiled=True)  30.6 us
    squeeze x8, local copies, waits for them, and re-layouts, run_block(): block_state[1]  13.4 us
    unnamed x4, local copies, waits for them, and re-layouts  13.3 us
    dynamic_update_slice x8, other arithmetic, visit(): return lax.dynamic_update_slice_in_dim(updated, result, start, 1)  11.7 us

commit v1 on v0

--- a/solution.py
+++ b/solution.py
@@ -121,7 +121,17 @@
     filtered = jnp.einsum(
         "mnj,mcn->mcj", table, spectrum * keep_mask[:, None, :], precision=highest
     )
-    piece = lax.all_gather(filtered, "lon", axis=0, tiled=True)
+    block_last = lax.axis_index("lon")
+    inter = lax.axis_size("lon")
+    d_next, p_next, placed = (inter, block_last, filtered.shape[0])
+    met_up, newest = (filtered, 1)
+    while newest < d_next:
+        everything = lax.ppermute(
+            met_up, "lon", [(at, (at - newest) % d_next) for at in range(d_next)]
+        )
+        met_up = jnp.concatenate([met_up, everything], axis=0)
+        newest = 2 * newest
+    piece = jnp.roll(met_up, p_next * placed, axis=0)
     modes = jnp.arange(piece.shape[0], dtype=jnp.int32)
     cosine_table, sine_table = wave_table(my_lons, modes, total_lon)
     factor = jnp.where(modes == 0, 1.0, 2.0).astype(jnp.float32)[:, None]

time: 387 us -> 365 us (0.943)
  blocking collectives: 69.3 us -> 38.8 us
  starting transfers between devices: 0 us -> 6.55 us
  loops' own time: 111 us -> 116 us
  local copies, waits for them, and re-layouts: 70.2 us -> 65.4 us
    all_gather x1 -> x0, blocking collectives: 30.6 us -> none  [shards(): piece = lax.all_gather(filtered, 'lon', axis=0, tiled=True)]
    ppermute x0 -> x3, starting transfers between devices: none -> 6.55 us  [shards(): lax.ppermute(met_up, 'lon', [(at, (at - newest) % d_next) for at in range...]
    dynamic_slice x8, local copies, waits for them, and re-layouts: 5.53 us -> 0.05 us  [visit(): count_rows = lax.dynamic_slice_in_dim(counts, start, block_rows, 0)]
    another operation x8, loops' own time: 48.8 us -> 53.4 us  [run_block(): lax.while_loop(unfinished, run_advance, (jnp.int32(0), block_state[0], bl...]
    unnamed x4 -> x12, local copies, waits for them, and re-layouts: 13.3 us -> 13.3 us
  transfers between devices with their start and end apart: 0 -> 3, of which waited for: 0 -> 2; matrix products, arithmetic and copies ran while one was open for 0% -> 3% of each run, Pallas kernels for 0% -> 0%
where the time goes in v1:
time: 365 us; the launch traced here: 363 us
  other arithmetic  130 us (36%)
  loops' own time  116 us (32%)
  local copies, waits for them, and re-layouts  65.4 us (18%)
  blocking collectives  38.8 us (11%)
  starting transfers between devices  6.55 us (2%)
    select_n x64, other arithmetic, substep(): jnp.where(active, moved_moist - condensed, moist)  91.4 us
    another operation x1, loops' own time, legendre(): lax.scan(legendre_advance, initial, jnp.arange(degrees, dtype=jnp.int32),...  62.1 us
    another operation x8, loops' own time, run_block(): lax.while_loop(unfinished, run_advance, (jnp.int32(0), block_state[0], bl...  53.4 us
    unnamed x1, blocking collectives  35.5 us
    squeeze x8, local copies, waits for them, and re-layouts, run_block(): block_state[1]  13.4 us
    unnamed x12, local copies, waits for them, and re-layouts  13.3 us
    dynamic_update_slice x8, other arithmetic, visit(): return lax.dynamic_update_slice_in_dim(updated, result, start, 1)  11.7 us
    add x64, other arithmetic, substep(): heated = theta + couple_gain * profile[None, None, :] * force[:, :, None]  9.97 us
  transfers between devices with their start and end apart: 3, of which 2 were waited for; matrix products, arithmetic and copies ran while one was open for 3% of the time, Pallas kernels for 0%

profile of v1, /device:TPU:8, one launch (start us, length us, event | category | flops | bytes accessed | tf_op | source)
XLA Modules:
  0.0 363.1 jit_solution(8892459899098874213)
XLA Ops:
  0.2 3.8 %slice_reduce_fusion = f32[32,64]{1,0:T(8,128)S(1)} fusion(f32[2,32,64,1024]{3,2,1,0:T(8,128)} %param.10), kind=kLoop, calls=%fused_computation.96 | loop fusion | flops 2095104 | bytes 8396800 | tf_op jit(solution)/shard_map/reduce_sum | solution.py:91
  5.0 35.5 %all-reduce = f32[96,2,64]{2,1,0:T(2,128)S(1)} all-reduce(f32[96,2,64]{2,1,0:T(2,128)S(1)} %copy.12), channel_id=2, replica_groups=mesh['grp'=2,'lon'=8,'lat'=2] {'lon'}, use_global_device_ids=true, to_apply=%region_1.2.clone | all-reduce | flops 12288 | bytes 98304
  40.5 82.5 %while.81 = (s32[]{:T(128)}, f32[12,64]{1,0:T(8,128)S(1)}, f32[12,64]{1,0:T(8,128)S(1)}, f32[12]{0:T(128)S(1)}, f32[12,8,12,64]{3,2,1,0:T(8,128)S(1)}, /*index=5...) while((s32[]{:T(128)}, f32[12,64]{1,0:T(8,128)S(1)}, ...), condition=%wide.region_4.5_spmd.clone.clone.clone, body=%wide.region_3.4_spmd.clone.clone.clone.sunk | while | flops 108922 | bytes 421596 | solution.py:35
  125.6 3.3 psum.7
  130.5 12.0 %copy.57 = f32[2,32,64,1024]{3,2,1,0:T(8,128)} copy(f32[2,32,64,1024]{3,2,1,0:T(8,128)} %param.10) | data formatting | bytes 33554432
  142.9 3.3 collective-permute-start.1
  146.2 1.5 collective-permute-done.1
  147.7 3.2 collective-permute-start.2
  151.0 2.1 collective-permute-done.2
  153.8 209.4 %while.80 = (s32[]{:T(128)}, f32[2,32,64,1024]{3,2,1,0:T(8,128)}, f32[2,32,64,1024]{3,2,1,0:T(8,128)}, s32[8]{0:T(128)S(1)}, f32[32,64]{1,0:T(8,128)S(1)}, /*ind...) while((s32[]{:T(128)}, f32[2,32,64,1024]{3,2,1,0:T(8,128)}, ...), condition=%wide.region_11.12_spmd.clone, body=%wide.region_8.11_spmd.clone.sunk | while | flops 6817033 | bytes 18993312 | solution.py:158
  154.6 1.7 dynamic-slice_bitcast_fusion.3
  156.3 22.3 %while.82 = (s32[]{:T(128)}, f32[4,64,1024]{2,1,0:T(8,128)S(1)}, f32[4,64,1024]{2,1,0:T(8,128)S(1)}, s32[]{:T(128)}, s32[4,64]{1,0:T(4,128)S(1)}, /*index=5*/f32...) while((s32[]{:T(128)}, f32[4,64,1024]{2,1,0:T(8,128)S(1)}, ...), condition=%wide.region_10.10_spmd, body=%wide.region_9.9_spmd.sunk | while | flops 6292738 | bytes 10583657 | solution.py:73
  178.5 1.5 maximum_dynamic-update-slice_fusion.2
  180.7 1.7 dynamic-slice_bitcast_fusion.3
  182.4 22.3 %while.82 = (s32[]{:T(128)}, f32[4,64,1024]{2,1,0:T(8,128)S(1)}, f32[4,64,1024]{2,1,0:T(8,128)S(1)}, s32[]{:T(128)}, s32[4,64]{1,0:T(4,128)S(1)}, /*index=5*/f32...) while((s32[]{:T(128)}, f32[4,64,1024]{2,1,0:T(8,128)S(1)}, ...), condition=%wide.region_10.10_spmd, body=%wide.region_9.9_spmd.sunk | while | flops 6292738 | bytes 10583657 | solution.py:73
  204.7 1.5 maximum_dynamic-update-slice_fusion.2
  206.9 1.7 dynamic-slice_bitcast_fusion.3
  208.6 22.3 %while.82 = (s32[]{:T(128)}, f32[4,64,1024]{2,1,0:T(8,128)S(1)}, f32[4,64,1024]{2,1,0:T(8,128)S(1)}, s32[]{:T(128)}, s32[4,64]{1,0:T(4,128)S(1)}, /*index=5*/f32...) while((s32[]{:T(128)}, f32[4,64,1024]{2,1,0:T(8,128)S(1)}, ...), condition=%wide.region_10.10_spmd, body=%wide.region_9.9_spmd.sunk | while | flops 6292738 | bytes 10583657 | solution.py:73
  230.9 1.5 maximum_dynamic-update-slice_fusion.2
  233.1 1.7 dynamic-slice_bitcast_fusion.3
  234.8 22.3 %while.82 = (s32[]{:T(128)}, f32[4,64,1024]{2,1,0:T(8,128)S(1)}, f32[4,64,1024]{2,1,0:T(8,128)S(1)}, s32[]{:T(128)}, s32[4,64]{1,0:T(4,128)S(1)}, /*index=5*/f32...) while((s32[]{:T(128)}, f32[4,64,1024]{2,1,0:T(8,128)S(1)}, ...), condition=%wide.region_10.10_spmd, body=%wide.region_9.9_spmd.sunk | while | flops 6292738 | bytes 10583657 | solution.py:73
  257.0 1.5 maximum_dynamic-update-slice_fusion.2
  259.2 1.7 dynamic-slice_bitcast_fusion.3
  260.9 22.3 %while.82 = (s32[]{:T(128)}, f32[4,64,1024]{2,1,0:T(8,128)S(1)}, f32[4,64,1024]{2,1,0:T(8,128)S(1)}, s32[]{:T(128)}, s32[4,64]{1,0:T(4,128)S(1)}, /*index=5*/f32...) while((s32[]{:T(128)}, f32[4,64,1024]{2,1,0:T(8,128)S(1)}, ...), condition=%wide.region_10.10_spmd, body=%wide.region_9.9_spmd.sunk | while | flops 6292738 | bytes 10583657 | solution.py:73
  283.2 1.5 maximum_dynamic-update-slice_fusion.2
  285.4 1.7 dynamic-slice_bitcast_fusion.3
  287.1 22.3 %while.82 = (s32[]{:T(128)}, f32[4,64,1024]{2,1,0:T(8,128)S(1)}, f32[4,64,1024]{2,1,0:T(8,128)S(1)}, s32[]{:T(128)}, s32[4,64]{1,0:T(4,128)S(1)}, /*index=5*/f32...) while((s32[]{:T(128)}, f32[4,64,1024]{2,1,0:T(8,128)S(1)}, ...), condition=%wide.region_10.10_spmd, body=%wide.region_9.9_spmd.sunk | while | flops 6292738 | bytes 10583657 | solution.py:73
  309.4 1.5 maximum_dynamic-update-slice_fusion.2
  311.6 1.7 dynamic-slice_bitcast_fusion.3
  313.3 22.3 %while.82 = (s32[]{:T(128)}, f32[4,64,1024]{2,1,0:T(8,128)S(1)}, f32[4,64,1024]{2,1,0:T(8,128)S(1)}, s32[]{:T(128)}, s32[4,64]{1,0:T(4,128)S(1)}, /*index=5*/f32...) while((s32[]{:T(128)}, f32[4,64,1024]{2,1,0:T(8,128)S(1)}, ...), condition=%wide.region_10.10_spmd, body=%wide.region_9.9_spmd.sunk | while | flops 6292738 | bytes 10583657 | solution.py:73
  337.7 1.7 dynamic-slice_bitcast_fusion.3
  339.4 22.3 %while.82 = (s32[]{:T(128)}, f32[4,64,1024]{2,1,0:T(8,128)S(1)}, f32[4,64,1024]{2,1,0:T(8,128)S(1)}, s32[]{:T(128)}, s32[4,64]{1,0:T(4,128)S(1)}, /*index=5*/f32...) while((s32[]{:T(128)}, f32[4,64,1024]{2,1,0:T(8,128)S(1)}, ...), condition=%wide.region_10.10_spmd, body=%wide.region_9.9_spmd.sunk | while | flops 6292738 | bytes 10583657 | solution.py:73
  (957 shorter events, 159.7 us)
Async XLA Ops:
  130.4 12.4 %collective-permute-start = (f32[12,2,64]{2,1,0:T(2,128)S(1)}, f32[12,2,64]{2,1,0:T(2,128)S(1)}, u32[]{:S(2)}, u32[]{:S(2)}) collective-permute-start(f32[12,2,64]{2,1,0:T(2,128)S(1)} %get-tuple-element.757), channel_id=1, source_target_pairs={{0,14},{2,0},{4,2},{6,4},{8,6},{10,8},{12,10},{14,12},{1,15},{3,1}... | collective-permute-start | bytes 18440 | tf_op jit(solution)/shard_map/ppermute | solution.py:129
  130.5 12.0 %copy-start = (s32[32,64]{1,0:T(8,128)S(1)}, s32[32,64]{1,0:T(8,128)}, u32[]{:S(2)}) copy-start(s32[32,64]{1,0:T(8,128)} %param.11) | copy-start | bytes 24580
  130.5 23.3 %copy-start.1 = (f32[32]{0:T(128)S(1)}, f32[32]{0:T(128)}, u32[]{:S(2)}) copy-start(f32[32]{0:T(128)} %param.12) | copy-start | bytes 388
  142.9 4.8 %collective-permute-start.1 = (f32[24,2,64]{2,1,0:T(2,128)S(1)}, f32[24,2,64]{2,1,0:T(2,128)S(1)}, u32[]{:S(2)}, u32[]{:S(2)}) collective-permute-start(f32[24,2,64]{2,1,0:T(2,128)S(1)} %pad_maximum_fusion.1), channel_id=1, source_target_pairs={{0,12},{2,14},{4,0},{6,2},{8,4},{10,6},{12,8},{14,10},{1,13},{3,15... | collective-permute-start | bytes 36872 | tf_op jit(solution)/shard_map/ppermute | solution.py:129
  147.7 5.3 %collective-permute-start.2 = (f32[48,2,64]{2,1,0:T(2,128)S(1)}, f32[48,2,64]{2,1,0:T(2,128)S(1)}, u32[]{:S(2)}, u32[]{:S(2)}) collective-permute-start(f32[48,2,64]{2,1,0:T(2,128)S(1)} %pad_maximum_fusion), channel_id=1, source_target_pairs={{0,8},{2,10},{4,12},{6,14},{8,0},{10,2},{12,4},{14,6},{1,9},{3,11}... | collective-permute-start | bytes 73736 | tf_op jit(solution)/shard_map/ppermute | solution.py:129
